TPU v7x, 32 devices: a whole 2x2x4 slice. The times are simulated.
32 devices in a mesh: batch: 8 (over z, y), head: 4 (over x, core).
Axes of the slice: x: 2, y: 2, z: 4, core: 2. Of those that a mesh axis runs over, the one named last changes fastest.
Arguments:
- tokens: bfloat16 [20480, 768], P(('batch', 'head')), may hold values from -6 to 6
- pass_ids: int32 [20480], P(('batch', 'head')), may hold values from 0 to 4
- segment_ids: int32 [16, 1280], P('batch'), may hold values from 0 to 3, never falling along the last dimension, each value on 1 to 640 neighbouring positions
- pass_embed: bfloat16 [5, 768], replicated, may hold values from -3 to 3
- norm1_gain: bfloat16 [768], replicated, may hold values from 0.5 to 1.5
- norm1_shift: bfloat16 [768], replicated, may hold values from -1 to 1
- qkv_weight: bfloat16 [768, 2304], replicated, may hold values from -0.21875 to 0.21875
- qv_bias: bfloat16 [2, 768], replicated, may hold values from -1 to 1
- out_weight: bfloat16 [768, 768], replicated, may hold values from -0.625 to 0.625
- out_bias: bfloat16 [768], replicated, may hold values from -1 to 1
- norm2_gain: bfloat16 [768], replicated, may hold values from 0.5 to 1.5
- norm2_shift: bfloat16 [768], replicated, may hold values from -1 to 1
- up_weight: bfloat16 [768, 3072], replicated, may hold values from -0.21875 to 0.21875
- up_bias: bfloat16 [3072], replicated, may hold values from -1 to 1
- down_weight: bfloat16 [3072, 768], replicated, may hold values from -0.109375 to 0.109375
- down_bias: bfloat16 [768], replicated, may hold values from -1 to 1
- cotangent: bfloat16 [20480, 768], P(('batch', 'head')), may hold values from -6 to 6
Outputs:
- mixed: bfloat16 [20480, 768], P(('batch', 'head'))
- input_grad: float32 [20480, 768], P(('batch', 'head'))
- pass_embed_grad: float32 [5, 768], P(None, ('batch', 'head'))
- norm1_gain_grad: float32 [768], P(('batch', 'head'))
- norm1_shift_grad: float32 [768], P(('batch', 'head'))
- qkv_weight_grad: float32 [768, 2304], P(None, ('batch', 'head'))
- qv_bias_grad: float32 [2, 768], P(None, ('batch', 'head'))
- out_weight_grad: float32 [768, 768], P(None, ('batch', 'head'))
- out_bias_grad: float32 [768], P(('batch', 'head'))
- norm2_gain_grad: float32 [768], P(('batch', 'head'))
- norm2_shift_grad: float32 [768], P(('batch', 'head'))
- up_weight_grad: float32 [768, 3072], P(None, ('batch', 'head'))
- up_bias_grad: float32 [3072], P(('batch', 'head'))
- down_weight_grad: float32 [3072, 768], P(None, ('batch', 'head'))
- down_bias_grad: float32 [768], P(('batch', 'head'))
Inputs may be any that keep to these rules, and one draw needn't show every extreme that they name: `segment_ids`: along a sequence the ids never fall; a segment holds at most 640 tokens and one holds exactly that many.
All inputs are finite; a program needn't handle non-finite values.
Results may differ from a plain program's by a relative error of at most 0.0095.
Values may be sent and summed in bfloat16 or wider, within the bound.
No kernel may reach another device: no remote copies, remote signals or barrier semaphores. Data moves between devices by JAX's collectives and lax.ppermute only.
A program may use at most 192 MiB of HBM per device.

v0:
```python
import jax
import jax.numpy as jnp
from jax import lax
from jax.sharding import PartitionSpec as P

HEAD_DIM = 64
SEQ_LEN = 1280


def layer_norm(values, gain, shift):
    center = values - jnp.mean(values, -1, keepdims=True)
    spread = jnp.mean(center * center, -1, keepdims=True)
    return center * lax.rsqrt(spread + 1e-05) * gain + shift


def masked_scores(q_rows, k_rows, seg_row):
    scores = jnp.einsum("qhd,khd->hqk", q_rows, k_rows, preferred_element_type=jnp.float32) * 0.125
    places = jnp.arange(q_rows.shape[0])
    allowed = (places[:, None] >= places[None, :]) & (seg_row[:, None] == seg_row[None, :])
    return jnp.where(allowed[None], scores, -1e30)


def attend_forward(inputs):
    q_rows, k_rows, v_rows, seg_row = inputs
    scores = masked_scores(q_rows, k_rows, seg_row)
    row_max = jnp.max(scores, -1, keepdims=True)
    raw_weights = jnp.exp(scores - row_max)
    row_sum = jnp.sum(raw_weights, -1, keepdims=True)
    probability = raw_weights / row_sum
    attended = jnp.einsum(
        "hqk,khd->qhd", probability.astype(jnp.bfloat16), v_rows, preferred_element_type=jnp.float32
    )
    return (attended.astype(jnp.bfloat16), (row_max + jnp.log(row_sum))[..., 0])


def attend_backward(inputs):
    q_rows, k_rows, v_rows, seg_row, log_sums, grad_rows = inputs
    scores = masked_scores(q_rows, k_rows, seg_row)
    probability = jnp.exp(scores - log_sums[..., None])
    grad_probs = jnp.einsum("qhd,khd->hqk", grad_rows, v_rows, preferred_element_type=jnp.float32)
    center = jnp.sum(probability * grad_probs, -1, keepdims=True)
    grad_scores = (probability * (grad_probs - center)).astype(jnp.bfloat16)
    grad_values = jnp.einsum(
        "hqk,qhd->khd",
        probability.astype(jnp.bfloat16),
        grad_rows,
        preferred_element_type=jnp.float32,
    )
    grad_queries = (
        jnp.einsum("hqk,khd->qhd", grad_scores, k_rows, preferred_element_type=jnp.float32) * 0.125
    )
    grad_keys = (
        jnp.einsum("hqk,qhd->khd", grad_scores, q_rows, preferred_element_type=jnp.float32) * 0.125
    )
    return (
        grad_queries.astype(jnp.bfloat16),
        grad_keys.astype(jnp.bfloat16),
        grad_values.astype(jnp.bfloat16),
    )


def on_device(
    tokens,
    pass_ids,
    segment_ids,
    pass_embed,
    norm1_gain,
    norm1_shift,
    qkv_weight,
    qv_bias,
    out_weight,
    out_bias,
    norm2_gain,
    norm2_shift,
    up_weight,
    up_bias,
    down_weight,
    down_bias,
    cotangent,
):
    rows_dev = tokens.shape[0]
    width = tokens.shape[1]
    groups = lax.axis_size("head")
    local = width // groups
    head_count = local // HEAD_DIM
    group_rows = rows_dev * groups
    seq_count = group_rows // SEQ_LEN
    gain_one = norm1_gain.astype(jnp.float32)
    shift_one = norm1_shift.astype(jnp.float32)
    gain_two = norm2_gain.astype(jnp.float32)
    shift_two = norm2_shift.astype(jnp.float32)
    one_hot = (pass_ids[:, None] == jnp.arange(pass_embed.shape[0])[None, :]).astype(jnp.float32)
    table = pass_embed.astype(jnp.float32)
    hidden = tokens.astype(jnp.float32) + jnp.dot(
        one_hot, table, precision=lax.Precision.HIGHEST, preferred_element_type=jnp.float32
    )
    normed = layer_norm(hidden, gain_one, shift_one).astype(jnp.bfloat16)
    bias_full = jnp.concatenate(
        [
            qv_bias[0].astype(jnp.float32),
            jnp.zeros((width,), jnp.float32),
            qv_bias[1].astype(jnp.float32),
        ]
    )
    joined = (jnp.dot(normed, qkv_weight, preferred_element_type=jnp.float32) + bias_full).astype(
        jnp.bfloat16
    )
    grouped = joined.reshape(rows_dev, 3, groups, local)
    arrived = lax.all_to_all(grouped, "head", split_axis=2, concat_axis=0, tiled=True).reshape(
        group_rows, 3 * local
    )
    q_heads = arrived[:, :local].reshape(seq_count, SEQ_LEN, head_count, HEAD_DIM)
    k_heads = arrived[:, local : 2 * local].reshape(seq_count, SEQ_LEN, head_count, HEAD_DIM)
    v_heads = arrived[:, 2 * local :].reshape(seq_count, SEQ_LEN, head_count, HEAD_DIM)
    outputs, log_sums = lax.map(attend_forward, (q_heads, k_heads, v_heads, segment_ids))
    attended = outputs.reshape(group_rows, local)
    mixed_heads = lax.all_to_all(attended, "head", split_axis=0, concat_axis=1, tiled=True)
    after_attn = (
        hidden
        + jnp.dot(mixed_heads, out_weight, preferred_element_type=jnp.float32)
        + out_bias.astype(jnp.float32)
    )
    normed_two = layer_norm(after_attn, gain_two, shift_two).astype(jnp.bfloat16)
    pre_act = jnp.dot(normed_two, up_weight, preferred_element_type=jnp.float32) + up_bias.astype(
        jnp.float32
    )
    activated = jax.nn.gelu(pre_act, approximate=True).astype(jnp.bfloat16)
    result = (
        after_attn
        + jnp.dot(activated, down_weight, preferred_element_type=jnp.float32)
        + down_bias.astype(jnp.float32)
    ).astype(jnp.bfloat16)
    grad_out = cotangent.astype(jnp.float32)
    down_grad = jnp.einsum("nf,nd->fd", activated, cotangent, preferred_element_type=jnp.float32)
    down_bias_grad = jnp.sum(grad_out, 0)
    grad_act = jnp.einsum("nd,fd->nf", cotangent, down_weight, preferred_element_type=jnp.float32)
    gelu_value, gelu_pull = jax.vjp(lambda inner: jax.nn.gelu(inner, approximate=True), pre_act)
    grad_pre = gelu_pull(grad_act)[0].astype(jnp.bfloat16)
    up_grad = jnp.einsum("nd,nf->df", normed_two, grad_pre, preferred_element_type=jnp.float32)
    up_bias_grad = jnp.sum(grad_pre.astype(jnp.float32), 0)
    grad_normed_two = jnp.einsum(
        "nf,df->nd", grad_pre, up_weight, preferred_element_type=jnp.float32
    )
    norm_two_value, norm_two_pull = jax.vjp(layer_norm, after_attn, gain_two, shift_two)
    grad_resid, gain_two_grad, shift_two_grad = norm_two_pull(grad_normed_two)
    grad_after = grad_out + grad_resid
    grad_branch = grad_after.astype(jnp.bfloat16)
    out_grad = jnp.einsum("nd,ne->de", mixed_heads, grad_branch, preferred_element_type=jnp.float32)
    out_bias_grad = jnp.sum(grad_branch.astype(jnp.float32), 0)
    grad_mixed = jnp.einsum(
        "ne,de->nd", grad_branch, out_weight, preferred_element_type=jnp.float32
    ).astype(jnp.bfloat16)
    grad_attended = lax.all_to_all(
        grad_mixed, "head", split_axis=1, concat_axis=0, tiled=True
    ).reshape(seq_count, SEQ_LEN, head_count, HEAD_DIM)
    grad_queries, grad_keys, grad_values = lax.map(
        attend_backward, (q_heads, k_heads, v_heads, segment_ids, log_sums, grad_attended)
    )
    grad_stack = jnp.stack(
        [
            grad_queries.reshape(group_rows, local),
            grad_keys.reshape(group_rows, local),
            grad_values.reshape(group_rows, local),
        ],
        1,
    )
    returned = lax.all_to_all(
        grad_stack.reshape(group_rows, 3, 1, local), "head", split_axis=0, concat_axis=2, tiled=True
    )
    grad_joined = returned.reshape(rows_dev, 3 * width)
    qkv_grad = jnp.einsum("nd,ne->de", normed, grad_joined, preferred_element_type=jnp.float32)
    bias_grad_full = jnp.sum(grad_joined.astype(jnp.float32), 0)
    grad_normed = jnp.einsum(
        "ne,de->nd", grad_joined, qkv_weight, preferred_element_type=jnp.float32
    )
    qv_grad = jnp.stack([bias_grad_full[:width], bias_grad_full[2 * width :]])
    norm_one_value, norm_one_pull = jax.vjp(layer_norm, hidden, gain_one, shift_one)
    grad_hidden_part, gain_one_grad, shift_one_grad = norm_one_pull(grad_normed)
    grad_hidden = grad_after + grad_hidden_part
    table_grad = jnp.einsum(
        "nr,nd->rd",
        one_hot,
        grad_hidden,
        precision=lax.Precision.HIGHEST,
        preferred_element_type=jnp.float32,
    )
    summed = (
        lax.psum_scatter(table_grad, ("batch", "head"), scatter_dimension=1, tiled=True),
        lax.psum_scatter(gain_one_grad, ("batch", "head"), scatter_dimension=0, tiled=True),
        lax.psum_scatter(shift_one_grad, ("batch", "head"), scatter_dimension=0, tiled=True),
        lax.psum_scatter(qkv_grad, ("batch", "head"), scatter_dimension=1, tiled=True),
        lax.psum_scatter(qv_grad, ("batch", "head"), scatter_dimension=1, tiled=True),
        lax.psum_scatter(out_grad, ("batch", "head"), scatter_dimension=1, tiled=True),
        lax.psum_scatter(out_bias_grad, ("batch", "head"), scatter_dimension=0, tiled=True),
        lax.psum_scatter(gain_two_grad, ("batch", "head"), scatter_dimension=0, tiled=True),
        lax.psum_scatter(shift_two_grad, ("batch", "head"), scatter_dimension=0, tiled=True),
        lax.psum_scatter(up_grad, ("batch", "head"), scatter_dimension=1, tiled=True),
        lax.psum_scatter(up_bias_grad, ("batch", "head"), scatter_dimension=0, tiled=True),
        lax.psum_scatter(down_grad, ("batch", "head"), scatter_dimension=1, tiled=True),
        lax.psum_scatter(down_bias_grad, ("batch", "head"), scatter_dimension=0, tiled=True),
    )
    return (
        result,
        grad_hidden,
        summed[0],
        summed[1],
        summed[2],
        summed[3],
        summed[4],
        summed[5],
        summed[6],
        summed[7],
        summed[8],
        summed[9],
        summed[10],
        summed[11],
        summed[12],
    )


def solution(mesh):
    in_specs = (
        P(("batch", "head"), None),
        P(("batch", "head")),
        P("batch", None),
        P(),
        P(),
        P(),
        P(),
        P(),
        P(),
        P(),
        P(),
        P(),
        P(),
        P(),
        P(),
        P(),
        P(("batch", "head"), None),
    )
    out_specs = (
        P(("batch", "head"), None),
        P(("batch", "head"), None),
        P(None, ("batch", "head")),
        P(("batch", "head")),
        P(("batch", "head")),
        P(None, ("batch", "head")),
        P(None, ("batch", "head")),
        P(None, ("batch", "head")),
        P(("batch", "head")),
        P(("batch", "head")),
        P(("batch", "head")),
        P(None, ("batch", "head")),
        P(("batch", "head")),
        P(None, ("batch", "head")),
        P(("batch", "head")),
    )
    return jax.shard_map(
        on_device, mesh=mesh, in_specs=in_specs, out_specs=out_specs, check_vma=False
    )
```

profile of v0, /device:TPU:0, one launch (start us, length us, event | category | flops | bytes accessed | tf_op | source)
XLA Modules:
  0.0 904.8 jit_solution(17227066216637011802)
XLA Ops:
  13.3 4.2 add_convert_fusion
  17.5 5.5 copy.131
  23.0 3.7 copy.132
  26.7 4.8 all-to-all-start
  31.6 35.5 %all-to-all-done = bf16[640,3,4,192]{0,3,1,2:T(8,128)(2,1)} async-done(((bf16[640,3,4,192]{0,3,1,2:T(8,128)(2,1)}), bf16[640,3,4,192]{0,3,1,2:T(8,128)(2,1)}, u32[]{:S(2)}, u32[]{:S(2)}) %all-to-all-start) | async-done | bytes 2949152 | tf_op jit(solution)/shard_map/all_to_all | solution.py:109
  67.1 4.1 copy.133
  91.1 71.0 %while.26 = (s32[]{:T(128)}, bf16[2,1280,3,64]{1,3,2,0:T(8,128)(2,1)}, f32[2,3,1280]{2,1,0:T(4,128)}, bf16[2,1280,3,64]{1,3,2,0:T(8,128)(2,1)}, s32[2,1280]{1,0:...) while((s32[]{:T(128)}, ...), condition=%wide.region_5.6_spmd, body=%wide.region_2.5_spmd.sunk | while | flops 1302769920 | bytes 64760020 | solution.py:115
  93.2 12.2 %fusion.116 = (f32[3,1280]{1,0:T(4,128)}, f32[3,1280,1280]{1,2,0:T(8,128)}) fusion(bf16[2,1280,3,64]{1,3,2,0:T(8,128)(2,1)} %get-tuple-element.407, s32[]{:T(128)S(6)} %copy.171, bf16[2,1280,3,64]{1,3,2,0:T(8,128)(2,1)} %get-tuple-element.406, pred[1280,1280]{0,1:T(8,128)(4,1)S(1)} %fusion.115), kind=kOutput, calls=%fused_computation.122.clone.1 | convolution fusion | flops 643887360 | bytes 22298624 | tf_op jit(solution)/shard_map/while/body/eval_jaxpr/qhd,khd->hqk/dot_general | solution.py:17
  105.4 9.8 %fusion.117 = f32[3,1280]{1,0:T(4,128)} fusion(f32[3,1280,1280]{1,2,0:T(8,128)} %get-tuple-element.371, f32[3,1280]{1,0:T(4,128)} %get-tuple-element.372), kind=kLoop, calls=%fused_computation.4.clone.1 | loop fusion | flops 9826560 | bytes 19691520 | tf_op jit(solution)/shard_map/while/body/eval_jaxpr/reduce_sum | solution.py:28
  115.2 10.9 %fusion.118 = bf16[2,1280,3,64]{1,3,2,0:T(8,128)(2,1)} fusion(bf16[2,1280,3,64]{1,3,2,0:T(8,128)(2,1)} %get-tuple-element.394, s32[]{:T(128)S(6)} %copy.171, f32[3,1280,1280]{1,2,0:T(8,128)} %get-tuple-element.371, f32[3,1280]{1,0:T(4,128)} %fusion.117, f32[3,1280]{1,0:T(4,128)} %get-tuple-element.372, bf16[2,1280,3,64]{1,3,2,0:T(8,128)(2,1)} %get-tuple-element.404), kind=kOutput, calls=%fused_computation.10.clone.1 | convolution fusion | flops 644136960 | bytes 20685824 | tf_op jit(solution)/shard_map/while/body/eval_jaxpr/hqk,khd->qhd/dot_general | solution.py:30
  128.6 12.2 %fusion.116 = (f32[3,1280]{1,0:T(4,128)}, f32[3,1280,1280]{1,2,0:T(8,128)}) fusion(bf16[2,1280,3,64]{1,3,2,0:T(8,128)(2,1)} %get-tuple-element.407, s32[]{:T(128)S(6)} %copy.171, bf16[2,1280,3,64]{1,3,2,0:T(8,128)(2,1)} %get-tuple-element.406, pred[1280,1280]{0,1:T(8,128)(4,1)S(1)} %fusion.115), kind=kOutput, calls=%fused_computation.122.clone.1 | convolution fusion | flops 643887360 | bytes 22298624 | tf_op jit(solution)/shard_map/while/body/eval_jaxpr/qhd,khd->hqk/dot_general | solution.py:17
  140.8 9.8 %fusion.117 = f32[3,1280]{1,0:T(4,128)} fusion(f32[3,1280,1280]{1,2,0:T(8,128)} %get-tuple-element.371, f32[3,1280]{1,0:T(4,128)} %get-tuple-element.372), kind=kLoop, calls=%fused_computation.4.clone.1 | loop fusion | flops 9826560 | bytes 19691520 | tf_op jit(solution)/shard_map/while/body/eval_jaxpr/reduce_sum | solution.py:28
  150.6 10.9 %fusion.118 = bf16[2,1280,3,64]{1,3,2,0:T(8,128)(2,1)} fusion(bf16[2,1280,3,64]{1,3,2,0:T(8,128)(2,1)} %get-tuple-element.394, s32[]{:T(128)S(6)} %copy.171, f32[3,1280,1280]{1,2,0:T(8,128)} %get-tuple-element.371, f32[3,1280]{1,0:T(4,128)} %fusion.117, f32[3,1280]{1,0:T(4,128)} %get-tuple-element.372, bf16[2,1280,3,64]{1,3,2,0:T(8,128)(2,1)} %get-tuple-element.404), kind=kOutput, calls=%fused_computation.10.clone.1 | convolution fusion | flops 644136960 | bytes 20685824 | tf_op jit(solution)/shard_map/while/body/eval_jaxpr/hqk,khd->qhd/dot_general | solution.py:30
  165.2 14.6 %all_to_all.51 = bf16[4,640,192]{1,0,2:T(4,128)(2,1)} reshape(bf16[2,1280,3,64]{1,0,3,2:T(2,128)(2,1)} %copy.137) | data formatting | bytes 1966080 | tf_op jit(solution)/shard_map/all_to_all | solution.py:117
  182.1 4.2 all-to-all-start.1
  190.9 9.3 %all-to-all-done.1 = bf16[4,640,192]{1,2,0:T(8,128)(2,1)} async-done(((bf16[4,640,192]{1,2,0:T(8,128)(2,1)}), bf16[4,640,192]{1,2,0:T(8,128)(2,1)}, u32[]{:S(2)}, u32[]{:S(2)}) %all-to-all-start.1) | async-done | bytes 983072 | tf_op jit(solution)/shard_map/all_to_all | solution.py:117
  200.2 3.4 fusion.73
  204.0 6.3 fusion.63
  210.4 8.6 convert_reduce_fusion
  219.0 4.1 multiply_reduce_fusion.1
  231.3 4.2 all-to-all-start.2
  235.6 4.0 fusion.74
  239.7 9.7 %all-to-all-done.2 = bf16[640,4,192]{0,2,1:T(8,128)(2,1)} async-done(((bf16[640,4,192]{0,2,1:T(8,128)(2,1)}), bf16[640,4,192]{0,2,1:T(8,128)(2,1)}, u32[]{:S(2)}, u32[]{:S(2)}) %all-to-all-start.2) | async-done | bytes 983072 | tf_op jit(solution)/shard_map/all_to_all | solution.py:153
  261.0 114.7 %while.27 = (s32[]{:T(128)}, bf16[2,1280,3,64]{1,3,2,0:T(8,128)(2,1)}, bf16[2,1280,3,64]{1,3,2,0:T(8,128)(2,1)}, bf16[2,1280,3,64]{1,3,2,0:T(8,128)(2,1)}, bf16[...) while((s32[]{:T(128)}, ...), condition=%wide.region_12.13_spmd, body=%wide.region_10.12_spmd.sunk | while | flops 3196104960 | bytes 195067312 | solution.py:156
  264.0 11.9 %fusion.127 = f32[3,1280,1280]{1,2,0:T(8,128)} fusion(f32[3,1280]{1,0:T(4,128)S(1)} %dynamic-slice_bitcast_fusion.2, pred[1280,1280]{0,1:T(8,128)(4,1)S(1)} %fusion.126, bf16[2,1280,3,64]{1,3,2,0:T(8,128)(2,1)} %get-tuple-element.437, s32[]{:T(128)S(6)} %copy.181, bf16[2,1280,3,64]{1,3,2,0:T(8,128)(2,1)} %get-tuple-element.435), kind=kOutput, calls=%fused_computation.23.clone.1 | convolution fusion | flops 643891200 | bytes 22298624 | tf_op jit(solution)/shard_map/while/body/eval_jaxpr/qhd,khd->hqk/dot_general | solution.py:17
  275.9 10.1 %fusion.130 = bf16[2,1280,3,64]{1,3,2,0:T(8,128)(2,1)S(1)} fusion(bf16[2,1280,3,64]{1,3,2,0:T(8,128)(2,1)S(1)} %copy-done.13, s32[]{:T(128)S(6)} %copy.181, f32[3,1280,1280]{1,2,0:T(8,128)} %fusion.127, bf16[2,1280,3,64]{1,3,2,0:T(8,128)(2,1)S(1)} %copy-done.1), kind=kOutput, calls=%fused_computation.36.clone.1 | convolution fusion | flops 634306560 | bytes 20644864 | tf_op jit(solution)/shard_map/while/body/eval_jaxpr/hqk,qhd->khd/dot_general | solution.py:43
  286.0 12.7 %multiply_reduce_fusion.8 = (f32[3,1280]{1,0:T(4,128)S(1)}, f32[3,1280,1280]{1,2,0:T(8,128)}) fusion(f32[3,1280,1280]{1,2,0:T(8,128)} %fusion.127, bf16[2,1280,3,64]{1,3,2,0:T(8,128)(2,1)S(1)} %copy-done.10, s32[]{:T(128)S(6)} %copy.181, bf16[2,1280,3,64]{1,3,2,0:T(8,128)(2,1)S(1)} %copy-done.1), kind=kOutput, calls=%fused_computation.25.clone.1 | convolution fusion | flops 638972160 | bytes 40321024 | tf_op jit(solution)/shard_map/while/body/eval_jaxpr/qhd,khd->hqk/dot_general | solution.py:40
  298.7 14.1 %multiply_convert_fusion.5 = bf16[3,1280,1280]{1,2,0:T(8,128)(2,1)S(1)} fusion(f32[3,1280,1280]{1,2,0:T(8,128)} %get-tuple-element.383, f32[3,1280,1280]{1,2,0:T(8,128)} %fusion.127, f32[3,1280]{1,0:T(4,128)S(1)} %get-tuple-element.384), kind=kLoop, calls=%fused_computation.24.clone.1 | loop fusion | flops 14745600 | bytes 49167360 | tf_op jit(solution)/shard_map/while/body/eval_jaxpr/convert_element_type | solution.py:42
  321.3 11.8 %fusion.127 = f32[3,1280,1280]{1,2,0:T(8,128)} fusion(f32[3,1280]{1,0:T(4,128)S(1)} %dynamic-slice_bitcast_fusion.2, pred[1280,1280]{0,1:T(8,128)(4,1)S(1)} %fusion.126, bf16[2,1280,3,64]{1,3,2,0:T(8,128)(2,1)} %get-tuple-element.437, s32[]{:T(128)S(6)} %copy.181, bf16[2,1280,3,64]{1,3,2,0:T(8,128)(2,1)} %get-tuple-element.435), kind=kOutput, calls=%fused_computation.23.clone.1 | convolution fusion | flops 643891200 | bytes 22298624 | tf_op jit(solution)/shard_map/while/body/eval_jaxpr/qhd,khd->hqk/dot_general | solution.py:17
  333.1 9.9 %fusion.130 = bf16[2,1280,3,64]{1,3,2,0:T(8,128)(2,1)S(1)} fusion(bf16[2,1280,3,64]{1,3,2,0:T(8,128)(2,1)S(1)} %copy-done.13, s32[]{:T(128)S(6)} %copy.181, f32[3,1280,1280]{1,2,0:T(8,128)} %fusion.127, bf16[2,1280,3,64]{1,3,2,0:T(8,128)(2,1)S(1)} %copy-done.1), kind=kOutput, calls=%fused_computation.36.clone.1 | convolution fusion | flops 634306560 | bytes 20644864 | tf_op jit(solution)/shard_map/while/body/eval_jaxpr/hqk,qhd->khd/dot_general | solution.py:43
  343.1 12.6 %multiply_reduce_fusion.8 = (f32[3,1280]{1,0:T(4,128)S(1)}, f32[3,1280,1280]{1,2,0:T(8,128)}) fusion(f32[3,1280,1280]{1,2,0:T(8,128)} %fusion.127, bf16[2,1280,3,64]{1,3,2,0:T(8,128)(2,1)S(1)} %copy-done.10, s32[]{:T(128)S(6)} %copy.181, bf16[2,1280,3,64]{1,3,2,0:T(8,128)(2,1)S(1)} %copy-done.1), kind=kOutput, calls=%fused_computation.25.clone.1 | convolution fusion | flops 638972160 | bytes 40321024 | tf_op jit(solution)/shard_map/while/body/eval_jaxpr/qhd,khd->hqk/dot_general | solution.py:40
  355.7 13.8 %multiply_convert_fusion.5 = bf16[3,1280,1280]{1,2,0:T(8,128)(2,1)S(1)} fusion(f32[3,1280,1280]{1,2,0:T(8,128)} %get-tuple-element.383, f32[3,1280,1280]{1,2,0:T(8,128)} %fusion.127, f32[3,1280]{1,0:T(4,128)S(1)} %get-tuple-element.384), kind=kLoop, calls=%fused_computation.24.clone.1 | loop fusion | flops 14745600 | bytes 49167360 | tf_op jit(solution)/shard_map/while/body/eval_jaxpr/convert_element_type | solution.py:42
  378.8 3.5 stack_reshape.11
  385.5 3.5 stack_reshape.9
  392.2 3.5 stack_reshape.10
  395.7 3.7 maximum_bitcast_fusion
  399.4 8.4 copy.148
  407.8 65.5 %all_to_all.65 = bf16[2560,3,1,192]{3,1,2,0:T(4,128)(2,1)} all-to-all(bf16[2560,3,1,192]{3,1,2,0:T(4,128)(2,1)} %copy.148), channel_id=1, replica_groups=mesh['batch'=8,'head'=4] {'head'}, dimensions={0} | all-to-all | bytes 5898240 | tf_op jit(solution)/shard_map/all_to_all | solution.py:167
  473.3 9.0 copy.157
  486.3 5.3 fusion.61
  491.7 11.4 %fusion.64 = f32[3072,768]{0,1:T(8,128)} fusion(bf16[640,768]{1,0:T(8,128)(2,1)} %param.37, f32[640,3072]{1,0:T(8,128)} %copy-done.52, f32[3072]{0:T(1024)} %convert_element_type.121), kind=kOutput, calls=%fused_computation.119 | convolution fusion | flops 3039559680 | bytes 18296832 | tf_op jit(solution)/shard_map/nf,nd->fd/dot_general | solution.py:134
  503.8 10.6 %fusion.62 = f32[768,3072]{0,1:T(8,128)} fusion(bf16[640,3072]{1,0:T(8,128)(2,1)} %copy-done.53, f32[640,768]{1,0:T(8,128)} %copy-done.11, f32[768]{0:T(1024)} %convert_element_type.119, f32[768]{0:T(1024)S(1)} %copy-done.43, f32[640]{0:T(1024)} %copy-done.44, f32[640]{0:T(1024)S(1)} %copy-done.31), kind=kOutput, calls=%fused_computation.117 | convolution fusion | flops 3022356480 | bytes 15346688 | tf_op jit(solution)/shard_map/nd,nf->df/dot_general | solution.py:139
  515.1 11.6 %add_convert_fusion.1 = bf16[640,768]{1,0:T(8,128)(2,1)} fusion(f32[640,768]{1,0:T(8,128)} %copy-done.11, bf16[3072,768]{1,0:T(8,128)(2,1)} %param.35, f32[768]{0:T(1024)S(1)} %convert_element_type.123, f32[640,3072]{1,0:T(8,128)} %copy-done.52, f32[3072]{0:T(1024)} %convert_element_type.121), kind=kOutput, calls=%fused_computation.87 | convolution fusion | flops 3041034240 | bytes 15547392 | tf_op jit(solution)/shard_map/dot_general | solution.py:130
  532.8 6.7 multiply_reduce_fusion.2
  544.5 44.9 %all-reduce.9 = (f32[5,768]{1,0:T(8,128)}, f32[768]{0:T(1024)}, f32[768]{0:T(1024)}, f32[2,768]{1,0:T(2,128)}, f32[768]{0:T(1024)}, /*index=5*/f32[768]{0:T(1024)}, f32[768]{0:T(1024)}, f32[3072]{0:T(1024)}, f32[768]{0:T(1024)}) all-reduce(f32[5,768]{1,0:T(8,128)} %fusion.56, ...), channel_id=2, replica_groups=mesh['batch'=8,'head'=4] {'batch','head'}, use_global_device_ids=true, to_apply=%region_15.16.clone | all-reduce | flops 13056 | bytes 104448
  600.9 13.9 %reduce-scatter.7.cloned.1.call-done = f32[768,72]{0,1:T(8,128)} async-done(((f32[768,2304]{0,1:T(8,128)}), f32[768,72]{0,1:T(8,128)}) %reduce-scatter.7.cloned.1.call-update) | async-done | bytes 221200 | tf_op jit(solution)/shard_map/reduce_scatter | solution.py:191
  614.8 141.5 %reduce-scatter.13.cloned.1.call-done = f32[3072,24]{0,1:T(8,128)} async-done(((f32[3072,768]{0,1:T(8,128)}), f32[3072,24]{0,1:T(8,128)}) %reduce-scatter.13.cloned.1.call-update) | async-done | bytes 294928 | tf_op jit(solution)/shard_map/reduce_scatter | solution.py:199
  756.3 141.5 %reduce-scatter.11.cloned.1.call-done = f32[768,96]{0,1:T(8,128)} async-done(((f32[768,3072]{0,1:T(8,128)}), f32[768,96]{0,1:T(8,128)}) %reduce-scatter.11.cloned.1.call-update) | async-done | bytes 294928 | tf_op jit(solution)/shard_map/reduce_scatter | solution.py:197
  (237 shorter events, 115.3 us)
Async XLA Ops:
  7.2 6.1 copy-start
  8.0 4.7 copy-start.37
  26.7 40.4 %all-to-all-start = ((bf16[640,3,4,192]{0,3,1,2:T(8,128)(2,1)}), bf16[640,3,4,192]{0,3,1,2:T(8,128)(2,1)}, u32[]{:S(2)}, u32[]{:S(2)}) async-start(bf16[640,3,4,192]{0,3,1,2:T(8,128)(2,1)} %copy.132), calls=%async_computation | async-start | bytes 5898240 | tf_op jit(solution)/shard_map/all_to_all | solution.py:109
  82.2 8.9 copy-start.25
  115.2 10.9 %copy-start.22 = (f32[3,1280]{1,0:T(4,128)S(1)}, f32[3,1280]{1,0:T(4,128)}, u32[]{:S(2)}) copy-start(f32[3,1280]{1,0:T(4,128)} %get-tuple-element.372) | copy-start | bytes 46084 | tf_op jit(solution)/shard_map/while
  115.2 10.9 %copy-start.23 = (f32[3,1280]{1,0:T(4,128)S(1)}, f32[3,1280]{1,0:T(4,128)}, u32[]{:S(2)}) copy-start(f32[3,1280]{1,0:T(4,128)} %fusion.117) | copy-start | bytes 46084 | tf_op jit(solution)/shard_map/while
  115.2 10.9 %copy-start.26 = (f32[2,3,1280]{2,1,0:T(4,128)S(1)}, f32[2,3,1280]{2,1,0:T(4,128)}, u32[]{:S(2)}) copy-start(f32[2,3,1280]{2,1,0:T(4,128)} %get-tuple-element.395) | copy-start | bytes 92164 | tf_op jit(solution)/shard_map/while
  150.6 10.9 %copy-start.22 = (f32[3,1280]{1,0:T(4,128)S(1)}, f32[3,1280]{1,0:T(4,128)}, u32[]{:S(2)}) copy-start(f32[3,1280]{1,0:T(4,128)} %get-tuple-element.372) | copy-start | bytes 46084 | tf_op jit(solution)/shard_map/while
  150.6 10.9 %copy-start.23 = (f32[3,1280]{1,0:T(4,128)S(1)}, f32[3,1280]{1,0:T(4,128)}, u32[]{:S(2)}) copy-start(f32[3,1280]{1,0:T(4,128)} %fusion.117) | copy-start | bytes 46084 | tf_op jit(solution)/shard_map/while
  150.6 10.9 %copy-start.26 = (f32[2,3,1280]{2,1,0:T(4,128)S(1)}, f32[2,3,1280]{2,1,0:T(4,128)}, u32[]{:S(2)}) copy-start(f32[2,3,1280]{2,1,0:T(4,128)} %get-tuple-element.395) | copy-start | bytes 92164 | tf_op jit(solution)/shard_map/while
  182.1 18.0 %all-to-all-start.1 = ((bf16[4,640,192]{1,2,0:T(8,128)(2,1)}), bf16[4,640,192]{1,2,0:T(8,128)(2,1)}, u32[]{:S(2)}, u32[]{:S(2)}) async-start(bf16[4,640,192]{1,2,0:T(8,128)(2,1)} %copy.138), calls=%async_computation.1 | async-start | bytes 1966080 | tf_op jit(solution)/shard_map/all_to_all | solution.py:117
  187.1 36.0 %copy-start.42 = (f32[768]{0:T(1024)}, f32[768]{0:T(1024)S(1)}, u32[]{:S(2)}) copy-start(f32[768]{0:T(1024)S(1)} %convert_element_type.118) | copy-start | bytes 9220
  203.5 19.6 %copy-start.11 = (f32[640,768]{1,0:T(8,128)}, f32[640,768]{1,0:T(8,128)S(1)}, u32[]{:S(2)}) copy-start(f32[640,768]{1,0:T(8,128)S(1)} %get-tuple-element.270) | copy-start | bytes 5898244
  203.6 19.6 %copy-start.30 = (f32[640]{0:T(1024)}, f32[640]{0:T(1024)S(1)}, u32[]{:S(2)}) copy-start(f32[640]{0:T(1024)S(1)} %broadcast_multiply_fusion) | copy-start | bytes 7684
  203.6 6.8 slice-start.2
  204.0 19.2 %copy-start.44 = (f32[640]{0:T(1024)}, f32[640]{0:T(1024)S(1)}, u32[]{:S(2)}) copy-start(f32[640]{0:T(1024)S(1)} %fusion.60) | copy-start | bytes 7684
  204.0 6.4 copy-start.19
  204.0 6.4 copy-start.46
  204.0 6.4 slice-start.3
  204.0 15.0 %slice-start = ((s8[4718592]{0:T(1024)(128)(4,1)}), s8[4194304]{0:T(1024)(128)(4,1)S(1)}, s32[]{:S(2)}) async-start(s8[4718592]{0:T(1024)(128)(4,1)} %bitcast.169), calls=%async_computation.12 | async-start | bytes 8388608
  210.4 8.6 copy-start.52
  210.4 8.6 slice-start.1
  219.0 4.1 copy-start.53
  223.2 4.0 copy-start.51
  231.3 18.0 %all-to-all-start.2 = ((bf16[640,4,192]{0,2,1:T(8,128)(2,1)}), bf16[640,4,192]{0,2,1:T(8,128)(2,1)}, u32[]{:S(2)}, u32[]{:S(2)}) async-start(bf16[640,4,192]{0,2,1:T(8,128)(2,1)} %bitcast.166), calls=%async_computation.2 | async-start | bytes 1966080 | tf_op jit(solution)/shard_map/all_to_all | solution.py:153
  235.6 365.3 %reduce-scatter.9.cloned.1.call-start = ((), (), s32[]{:S(2)}) async-start(), calls=%async_computation.9 | async-start | bytes 2433024 | tf_op jit(solution)/shard_map/reduce_scatter | solution.py:193
  239.7 375.1 %reduce-scatter.7.cloned.1.call-start = ((), (), s32[]{:S(2)}) async-start(), calls=%async_computation.8 | async-start | bytes 7299072 | tf_op jit(solution)/shard_map/reduce_scatter | solution.py:191
  263.9 11.9 %copy-start.1 = (bf16[2,1280,3,64]{1,3,2,0:T(8,128)(2,1)S(1)}, bf16[2,1280,3,64]{1,3,2,0:T(8,128)(2,1)}, u32[]{:S(2)}) copy-start(bf16[2,1280,3,64]{1,3,2,0:T(8,128)(2,1)} %get-tuple-element.439) | copy-start | bytes 2949124 | tf_op jit(solution)/shard_map/while
  264.0 11.9 %copy-start.13 = (bf16[2,1280,3,64]{1,3,2,0:T(8,128)(2,1)S(1)}, bf16[2,1280,3,64]{1,3,2,0:T(8,128)(2,1)}, u32[]{:S(2)}) copy-start(bf16[2,1280,3,64]{1,3,2,0:T(8,128)(2,1)} %get-tuple-element.423) | copy-start | bytes 2949124 | tf_op jit(solution)/shard_map/while
  275.9 10.1 %copy-start.10 = (bf16[2,1280,3,64]{1,3,2,0:T(8,128)(2,1)S(1)}, bf16[2,1280,3,64]{1,3,2,0:T(8,128)(2,1)}, u32[]{:S(2)}) copy-start(bf16[2,1280,3,64]{1,3,2,0:T(8,128)(2,1)} %get-tuple-element.440) | copy-start | bytes 2949124 | tf_op jit(solution)/shard_map/while
  286.0 12.7 %copy-start.14 = (bf16[2,1280,3,64]{1,3,2,0:T(8,128)(2,1)}, bf16[2,1280,3,64]{1,3,2,0:T(8,128)(2,1)S(1)}, u32[]{:S(2)}) copy-start(bf16[2,1280,3,64]{1,3,2,0:T(8,128)(2,1)S(1)} %fusion.130) | copy-start | bytes 2949124 | tf_op jit(solution)/shard_map/while
  298.7 14.1 %copy-start.8 = (bf16[2,1280,3,64]{1,3,2,0:T(8,128)(2,1)S(1)}, bf16[2,1280,3,64]{1,3,2,0:T(8,128)(2,1)}, u32[]{:S(2)}) copy-start(bf16[2,1280,3,64]{1,3,2,0:T(8,128)(2,1)} %get-tuple-element.437) | copy-start | bytes 2949124 | tf_op jit(solution)/shard_map/while
  298.7 14.1 %copy-start.15 = (bf16[2,1280,3,64]{1,3,2,0:T(8,128)(2,1)S(1)}, bf16[2,1280,3,64]{1,3,2,0:T(8,128)(2,1)}, u32[]{:S(2)}) copy-start(bf16[2,1280,3,64]{1,3,2,0:T(8,128)(2,1)} %get-tuple-element.422) | copy-start | bytes 2949124 | tf_op jit(solution)/shard_map/while
  321.3 11.8 %copy-start.1 = (bf16[2,1280,3,64]{1,3,2,0:T(8,128)(2,1)S(1)}, bf16[2,1280,3,64]{1,3,2,0:T(8,128)(2,1)}, u32[]{:S(2)}) copy-start(bf16[2,1280,3,64]{1,3,2,0:T(8,128)(2,1)} %get-tuple-element.439) | copy-start | bytes 2949124 | tf_op jit(solution)/shard_map/while
  321.3 11.8 %copy-start.13 = (bf16[2,1280,3,64]{1,3,2,0:T(8,128)(2,1)S(1)}, bf16[2,1280,3,64]{1,3,2,0:T(8,128)(2,1)}, u32[]{:S(2)}) copy-start(bf16[2,1280,3,64]{1,3,2,0:T(8,128)(2,1)} %get-tuple-element.423) | copy-start | bytes 2949124 | tf_op jit(solution)/shard_map/while
  333.1 9.9 %copy-start.10 = (bf16[2,1280,3,64]{1,3,2,0:T(8,128)(2,1)S(1)}, bf16[2,1280,3,64]{1,3,2,0:T(8,128)(2,1)}, u32[]{:S(2)}) copy-start(bf16[2,1280,3,64]{1,3,2,0:T(8,128)(2,1)} %get-tuple-element.440) | copy-start | bytes 2949124 | tf_op jit(solution)/shard_map/while
  343.1 12.7 %copy-start.14 = (bf16[2,1280,3,64]{1,3,2,0:T(8,128)(2,1)}, bf16[2,1280,3,64]{1,3,2,0:T(8,128)(2,1)S(1)}, u32[]{:S(2)}) copy-start(bf16[2,1280,3,64]{1,3,2,0:T(8,128)(2,1)S(1)} %fusion.130) | copy-start | bytes 2949124 | tf_op jit(solution)/shard_map/while
  355.7 13.8 %copy-start.8 = (bf16[2,1280,3,64]{1,3,2,0:T(8,128)(2,1)S(1)}, bf16[2,1280,3,64]{1,3,2,0:T(8,128)(2,1)}, u32[]{:S(2)}) copy-start(bf16[2,1280,3,64]{1,3,2,0:T(8,128)(2,1)} %get-tuple-element.437) | copy-start | bytes 2949124 | tf_op jit(solution)/shard_map/while
  355.7 13.9 %copy-start.15 = (bf16[2,1280,3,64]{1,3,2,0:T(8,128)(2,1)S(1)}, bf16[2,1280,3,64]{1,3,2,0:T(8,128)(2,1)}, u32[]{:S(2)}) copy-start(bf16[2,1280,3,64]{1,3,2,0:T(8,128)(2,1)} %get-tuple-element.422) | copy-start | bytes 2949124 | tf_op jit(solution)/shard_map/while
  482.3 4.0 copy-start.38
  482.3 4.0 copy-start.40
  482.3 4.0 copy-start.48
  491.7 264.6 %reduce-scatter.13.cloned.1.call-start = ((), (), s32[]{:S(2)}) async-start(), calls=%async_computation.11 | async-start | bytes 9732096 | tf_op jit(solution)/shard_map/reduce_scatter | solution.py:199
  503.1 394.7 %reduce-scatter.11.cloned.1.call-start = ((), (), s32[]{:S(2)}) async-start(), calls=%async_computation.10 | async-start | bytes 9732096 | tf_op jit(solution)/shard_map/reduce_scatter | solution.py:197
  515.1 11.6 %copy-start.2 = (bf16[4,640,3,1,192]{1,0,4,2,3:T(4,128)(2,1)S(1)}, bf16[4,640,3,1,192]{1,0,4,2,3:T(4,128)(2,1)}, u32[]{:S(2)}) copy-start(bf16[4,640,3,1,192]{1,0,4,2,3:T(4,128)(2,1)} %copy.157) | copy-start | bytes 8847364
  532.7 6.7 copy-start.33
  532.7 6.8 copy-start.5
  532.8 6.8 copy-start.41
  (31 other events, 59.4 us)
Sparse Core Ops, SparseCore 0:
  242.2 102.1 reduce-scatter.8
  491.8 122.8 reduce-scatter.6
  621.2 135.0 reduce-scatter.12
  762.6 135.1 reduce-scatter.10
where the time goes:
time: 911 us; the launch traced here: 905 us
  waiting for transfers between devices  351 us (39%)
  matrix products  206 us (23%)
  local copies, waits for them, and re-layouts  136 us (15%)
  blocking collectives  110 us (12%)
  other arithmetic  71.1 us (8%)
  between operations  14.8 us (2%)
  starting transfers between devices  13.7 us (2%)
    reduce_scatter x1, waiting for transfers between devices, on_device(): lax.psum_scatter(down_grad, ('batch', 'head'), scatter_dimension=1, tiled...  142 us
    reduce_scatter x1, waiting for transfers between devices, on_device(): lax.psum_scatter(up_grad, ('batch', 'head'), scatter_dimension=1, tiled=T...  142 us
    all_to_all x1, blocking collectives, on_device(): lax.all_to_all(grad_stack.reshape(group_rows, 3, 1, local), 'head', split...  65.5 us
    dot_general x4, matrix products, masked_scores(): jnp.einsum('qhd,khd->hqk', q_rows, k_rows, preferred_element_type=jnp.flo...  48.1 us
    unnamed x1, blocking collectives  44.9 us
    all_to_all x1, waiting for transfers between devices, on_device(): lax.all_to_all(grouped, 'head', split_axis=2, concat_axis=0, tiled=True)  35.5 us
    convert_element_type x2, other arithmetic, attend_backward(): grad_scores = (probability * (grad_probs - center)).astype(jnp.bfloat16)  27.9 us
    dot_general x2, matrix products, attend_backward(): jnp.einsum('qhd,khd->hqk', grad_rows, v_rows, preferred_element_type=jnp....  25.3 us
  transfers between devices with their start and end apart: 7, of which 6 were waited for; matrix products, arithmetic and copies ran while one was open for 27% of the time, Pallas kernels for 0%

commit v1 on v0

--- a/solution.py
+++ b/solution.py
@@ -5,6 +5,17 @@
 
 HEAD_DIM = 64
 SEQ_LEN = 1280
+
+
+def split_up(x, dim, size):
+    before, after = (x.shape[:dim], x.shape[dim + 1 :])
+    return jnp.moveaxis(x.reshape(*before, size, -1, *after), dim, 0)
+
+
+def laid_out(pieces, dim):
+    shape = list(pieces.shape[1:])
+    shape[dim] *= pieces.shape[0]
+    return jnp.moveaxis(pieces, 0, dim).reshape(shape)
 
 
 def layer_norm(values, gain, shift):
@@ -164,9 +175,15 @@
         ],
         1,
     )
-    returned = lax.all_to_all(
-        grad_stack.reshape(group_rows, 3, 1, local), "head", split_axis=0, concat_axis=2, tiled=True
-    )
+    x = grad_stack.reshape(group_rows, 3, 1, local)
+    size, index = (lax.axis_size("head"), lax.axis_index("head"))
+    parts = split_up(x, 0, size)
+    outs = [parts[index]]
+    for step in range(1, size):
+        sent = parts[index ^ step]
+        outs.append(lax.ppermute(sent, "head", [(i, i ^ step) for i in range(size)]))
+    parts = jnp.stack(outs)[index ^ jnp.arange(size)]
+    returned = laid_out(parts, 2)
     grad_joined = returned.reshape(rows_dev, 3 * width)
     qkv_grad = jnp.einsum("nd,ne->de", normed, grad_joined, preferred_element_type=jnp.float32)
     bias_grad_full = jnp.sum(grad_joined.astype(jnp.float32), 0)

time: 911 us -> 872 us (0.957)
  blocking collectives: 110 us -> 44.5 us
  waiting for transfers between devices: 351 us -> 385 us
  local copies, waits for them, and re-layouts: 136 us -> 126 us
    all_to_all x1 -> x0, blocking collectives: 65.5 us -> none  [on_device(): lax.all_to_all(grad_stack.reshape(group_rows, 3, 1, local), 'head', split...]
    ppermute x0 -> x3, waiting for transfers between devices: none -> 29.8 us  [on_device(): lax.ppermute(sent, 'head', [(i, i ^ step) for i in range(size)])]
    all_to_all x2 -> x0, local copies, waits for them, and re-layouts: 11.4 us -> none  [on_device(): lax.all_to_all(grad_stack.reshape(group_rows, 3, 1, local), 'head', split...]
    all_to_all x2, local copies, waits for them, and re-layouts: 16.9 us -> 6.47 us  [on_device(): lax.all_to_all(attended, 'head', split_axis=0, concat_axis=1, tiled=True)]
    unnamed x98 -> x105, local copies, waits for them, and re-layouts: 20.5 us -> 24.2 us
  transfers between devices with their start and end apart: 7 -> 10, of which waited for: 6 -> 9; matrix products, arithmetic and copies ran while one was open for 27% -> 28% of each run, Pallas kernels for 0% -> 0%
where the time goes in v1:
time: 872 us; the launch traced here: 867 us
  waiting for transfers between devices  385 us (44%)
  matrix products  206 us (24%)
  local copies, waits for them, and re-layouts  126 us (14%)
  other arithmetic  73.6 us (8%)
  blocking collectives  44.5 us (5%)
  starting transfers between devices  16 us (2%)
  between operations  14.7 us (2%)
    reduce_scatter x1, waiting for transfers between devices, on_device(): lax.psum_scatter(down_grad, ('batch', 'head'), scatter_dimension=1, tiled...  142 us
    reduce_scatter x1, waiting for transfers between devices, on_device(): lax.psum_scatter(up_grad, ('batch', 'head'), scatter_dimension=1, tiled=T...  141 us
    dot_general x4, matrix products, masked_scores(): jnp.einsum('qhd,khd->hqk', q_rows, k_rows, preferred_element_type=jnp.flo...  48.1 us
    unnamed x1, blocking collectives  44.5 us
    all_to_all x1, waiting for transfers between devices, on_device(): lax.all_to_all(grouped, 'head', split_axis=2, concat_axis=0, tiled=True)  35.5 us
    ppermute x3, waiting for transfers between devices, on_device(): lax.ppermute(sent, 'head', [(i, i ^ step) for i in range(size)])  29.8 us
    convert_element_type x2, other arithmetic, attend_backward(): grad_scores = (probability * (grad_probs - center)).astype(jnp.bfloat16)  27.9 us
    dot_general x2, matrix products, attend_backward(): jnp.einsum('qhd,khd->hqk', grad_rows, v_rows, preferred_element_type=jnp....  25.4 us
  transfers between devices with their start and end apart: 10, of which 9 were waited for; matrix products, arithmetic and copies ran while one was open for 28% of the time, Pallas kernels for 0%

profile of v1, /device:TPU:0, one launch (start us, length us, event | category | flops | bytes accessed | tf_op | source)
XLA Modules:
  0.0 867.1 jit_solution(7099264817431570854)
XLA Ops:
  13.3 4.3 add_convert_fusion
  17.6 5.4 copy.65
  23.0 3.7 copy.66
  26.7 5.1 all-to-all-start
  31.8 35.5 %all-to-all-done = bf16[640,3,4,192]{0,3,1,2:T(8,128)(2,1)} async-done(((bf16[640,3,4,192]{0,3,1,2:T(8,128)(2,1)}), bf16[640,3,4,192]{0,3,1,2:T(8,128)(2,1)}, u32[]{:S(2)}, u32[]{:S(2)}) %all-to-all-start) | async-done | bytes 2949152 | tf_op jit(solution)/shard_map/all_to_all | solution.py:120
  67.4 4.1 copy.67
  91.4 70.9 %while.26 = (s32[]{:T(128)}, bf16[2,1280,3,64]{1,3,2,0:T(8,128)(2,1)}, f32[2,3,1280]{2,1,0:T(4,128)}, bf16[2,1280,3,64]{1,3,2,0:T(8,128)(2,1)}, s32[2,1280]{1,0:...) while((s32[]{:T(128)}, ...), condition=%wide.region_5.6_spmd, body=%wide.region_2.5_spmd.sunk | while | flops 1302769920 | bytes 64760020 | solution.py:126
  93.4 12.2 %fusion.116 = (f32[3,1280]{1,0:T(4,128)}, f32[3,1280,1280]{1,2,0:T(8,128)}) fusion(bf16[2,1280,3,64]{1,3,2,0:T(8,128)(2,1)} %get-tuple-element.360, s32[]{:T(128)S(6)} %copy.115, bf16[2,1280,3,64]{1,3,2,0:T(8,128)(2,1)} %get-tuple-element.359, pred[1280,1280]{0,1:T(8,128)(4,1)S(1)} %fusion.115), kind=kOutput, calls=%fused_computation.139.clone.1 | convolution fusion | flops 643887360 | bytes 22298624 | tf_op jit(solution)/shard_map/while/body/eval_jaxpr/qhd,khd->hqk/dot_general | solution.py:28
  105.6 9.8 %fusion.117 = f32[3,1280]{1,0:T(4,128)} fusion(f32[3,1280,1280]{1,2,0:T(8,128)} %get-tuple-element.324, f32[3,1280]{1,0:T(4,128)} %get-tuple-element.325), kind=kLoop, calls=%fused_computation.5.clone.1 | loop fusion | flops 9826560 | bytes 19691520 | tf_op jit(solution)/shard_map/while/body/eval_jaxpr/reduce_sum | solution.py:39
  115.4 10.9 %fusion.118 = bf16[2,1280,3,64]{1,3,2,0:T(8,128)(2,1)} fusion(bf16[2,1280,3,64]{1,3,2,0:T(8,128)(2,1)} %get-tuple-element.347, s32[]{:T(128)S(6)} %copy.115, f32[3,1280,1280]{1,2,0:T(8,128)} %get-tuple-element.324, f32[3,1280]{1,0:T(4,128)} %fusion.117, f32[3,1280]{1,0:T(4,128)} %get-tuple-element.325, bf16[2,1280,3,64]{1,3,2,0:T(8,128)(2,1)} %get-tuple-element.357), kind=kOutput, calls=%fused_computation.11.clone.1 | convolution fusion | flops 644136960 | bytes 20685824 | tf_op jit(solution)/shard_map/while/body/eval_jaxpr/hqk,khd->qhd/dot_general | solution.py:41
  128.8 12.2 %fusion.116 = (f32[3,1280]{1,0:T(4,128)}, f32[3,1280,1280]{1,2,0:T(8,128)}) fusion(bf16[2,1280,3,64]{1,3,2,0:T(8,128)(2,1)} %get-tuple-element.360, s32[]{:T(128)S(6)} %copy.115, bf16[2,1280,3,64]{1,3,2,0:T(8,128)(2,1)} %get-tuple-element.359, pred[1280,1280]{0,1:T(8,128)(4,1)S(1)} %fusion.115), kind=kOutput, calls=%fused_computation.139.clone.1 | convolution fusion | flops 643887360 | bytes 22298624 | tf_op jit(solution)/shard_map/while/body/eval_jaxpr/qhd,khd->hqk/dot_general | solution.py:28
  141.0 9.8 %fusion.117 = f32[3,1280]{1,0:T(4,128)} fusion(f32[3,1280,1280]{1,2,0:T(8,128)} %get-tuple-element.324, f32[3,1280]{1,0:T(4,128)} %get-tuple-element.325), kind=kLoop, calls=%fused_computation.5.clone.1 | loop fusion | flops 9826560 | bytes 19691520 | tf_op jit(solution)/shard_map/while/body/eval_jaxpr/reduce_sum | solution.py:39
  150.7 10.9 %fusion.118 = bf16[2,1280,3,64]{1,3,2,0:T(8,128)(2,1)} fusion(bf16[2,1280,3,64]{1,3,2,0:T(8,128)(2,1)} %get-tuple-element.347, s32[]{:T(128)S(6)} %copy.115, f32[3,1280,1280]{1,2,0:T(8,128)} %get-tuple-element.324, f32[3,1280]{1,0:T(4,128)} %fusion.117, f32[3,1280]{1,0:T(4,128)} %get-tuple-element.325, bf16[2,1280,3,64]{1,3,2,0:T(8,128)(2,1)} %get-tuple-element.357), kind=kOutput, calls=%fused_computation.11.clone.1 | convolution fusion | flops 644136960 | bytes 20685824 | tf_op jit(solution)/shard_map/while/body/eval_jaxpr/hqk,khd->qhd/dot_general | solution.py:41
  165.4 4.2 all_to_all.40
  171.9 4.2 all-to-all-start.1
  180.7 9.3 %all-to-all-done.1 = bf16[4,640,192]{1,2,0:T(8,128)(2,1)} async-done(((bf16[4,640,192]{1,2,0:T(8,128)(2,1)}), bf16[4,640,192]{1,2,0:T(8,128)(2,1)}, u32[]{:S(2)}, u32[]{:S(2)}) %all-to-all-start.1) | async-done | bytes 983072 | tf_op jit(solution)/shard_map/all_to_all | solution.py:128
  193.8 6.3 fusion.64
  200.2 8.6 convert_reduce_fusion
  208.7 4.1 multiply_reduce_fusion.1
  221.1 4.2 all-to-all-start.2
  225.4 4.0 fusion.74
  229.5 9.6 %all-to-all-done.2 = bf16[640,4,192]{0,2,1:T(8,128)(2,1)} async-done(((bf16[640,4,192]{0,2,1:T(8,128)(2,1)}), bf16[640,4,192]{0,2,1:T(8,128)(2,1)}, u32[]{:S(2)}, u32[]{:S(2)}) %all-to-all-start.2) | async-done | bytes 983072 | tf_op jit(solution)/shard_map/all_to_all | solution.py:164
  250.7 114.7 %while.27 = (s32[]{:T(128)}, bf16[2,1280,3,64]{1,3,2,0:T(8,128)(2,1)}, bf16[2,1280,3,64]{1,3,2,0:T(8,128)(2,1)}, bf16[2,1280,3,64]{1,3,2,0:T(8,128)(2,1)}, bf16[...) while((s32[]{:T(128)}, ...), condition=%wide.region_12.13_spmd, body=%wide.region_10.12_spmd.sunk | while | flops 3196104960 | bytes 195067312 | solution.py:167
  253.4 11.9 %fusion.127 = f32[3,1280,1280]{1,2,0:T(8,128)} fusion(f32[3,1280]{1,0:T(4,128)S(1)} %dynamic-slice_bitcast_fusion.2, pred[1280,1280]{0,1:T(8,128)(4,1)S(1)} %fusion.126, bf16[2,1280,3,64]{1,3,2,0:T(8,128)(2,1)} %get-tuple-element.390, s32[]{:T(128)S(6)} %copy.125, bf16[2,1280,3,64]{1,3,2,0:T(8,128)(2,1)} %get-tuple-element.388), kind=kOutput, calls=%fused_computation.24.clone.1 | convolution fusion | flops 643891200 | bytes 22298624 | tf_op jit(solution)/shard_map/while/body/eval_jaxpr/qhd,khd->hqk/dot_general | solution.py:28
  265.3 10.1 %fusion.130 = bf16[2,1280,3,64]{1,3,2,0:T(8,128)(2,1)S(1)} fusion(bf16[2,1280,3,64]{1,3,2,0:T(8,128)(2,1)S(1)} %copy-done.14, s32[]{:T(128)S(6)} %copy.125, f32[3,1280,1280]{1,2,0:T(8,128)} %fusion.127, bf16[2,1280,3,64]{1,3,2,0:T(8,128)(2,1)S(1)} %copy-done.2), kind=kOutput, calls=%fused_computation.37.clone.1 | convolution fusion | flops 634306560 | bytes 20644864 | tf_op jit(solution)/shard_map/while/body/eval_jaxpr/hqk,qhd->khd/dot_general | solution.py:54
  275.5 12.7 %multiply_reduce_fusion.8 = (f32[3,1280]{1,0:T(4,128)S(1)}, f32[3,1280,1280]{1,2,0:T(8,128)}) fusion(f32[3,1280,1280]{1,2,0:T(8,128)} %fusion.127, bf16[2,1280,3,64]{1,3,2,0:T(8,128)(2,1)S(1)} %copy-done.10, s32[]{:T(128)S(6)} %copy.125, bf16[2,1280,3,64]{1,3,2,0:T(8,128)(2,1)S(1)} %copy-done.2), kind=kOutput, calls=%fused_computation.26.clone.1 | convolution fusion | flops 638972160 | bytes 40321024 | tf_op jit(solution)/shard_map/while/body/eval_jaxpr/qhd,khd->hqk/dot_general | solution.py:51
  288.2 14.1 %multiply_convert_fusion.5 = bf16[3,1280,1280]{1,2,0:T(8,128)(2,1)S(1)} fusion(f32[3,1280,1280]{1,2,0:T(8,128)} %get-tuple-element.336, f32[3,1280,1280]{1,2,0:T(8,128)} %fusion.127, f32[3,1280]{1,0:T(4,128)S(1)} %get-tuple-element.337), kind=kLoop, calls=%fused_computation.25.clone.1 | loop fusion | flops 14745600 | bytes 49167360 | tf_op jit(solution)/shard_map/while/body/eval_jaxpr/convert_element_type | solution.py:53
  310.8 11.8 %fusion.127 = f32[3,1280,1280]{1,2,0:T(8,128)} fusion(f32[3,1280]{1,0:T(4,128)S(1)} %dynamic-slice_bitcast_fusion.2, pred[1280,1280]{0,1:T(8,128)(4,1)S(1)} %fusion.126, bf16[2,1280,3,64]{1,3,2,0:T(8,128)(2,1)} %get-tuple-element.390, s32[]{:T(128)S(6)} %copy.125, bf16[2,1280,3,64]{1,3,2,0:T(8,128)(2,1)} %get-tuple-element.388), kind=kOutput, calls=%fused_computation.24.clone.1 | convolution fusion | flops 643891200 | bytes 22298624 | tf_op jit(solution)/shard_map/while/body/eval_jaxpr/qhd,khd->hqk/dot_general | solution.py:28
  322.6 9.9 %fusion.130 = bf16[2,1280,3,64]{1,3,2,0:T(8,128)(2,1)S(1)} fusion(bf16[2,1280,3,64]{1,3,2,0:T(8,128)(2,1)S(1)} %copy-done.14, s32[]{:T(128)S(6)} %copy.125, f32[3,1280,1280]{1,2,0:T(8,128)} %fusion.127, bf16[2,1280,3,64]{1,3,2,0:T(8,128)(2,1)S(1)} %copy-done.2), kind=kOutput, calls=%fused_computation.37.clone.1 | convolution fusion | flops 634306560 | bytes 20644864 | tf_op jit(solution)/shard_map/while/body/eval_jaxpr/hqk,qhd->khd/dot_general | solution.py:54
  332.5 12.7 %multiply_reduce_fusion.8 = (f32[3,1280]{1,0:T(4,128)S(1)}, f32[3,1280,1280]{1,2,0:T(8,128)}) fusion(f32[3,1280,1280]{1,2,0:T(8,128)} %fusion.127, bf16[2,1280,3,64]{1,3,2,0:T(8,128)(2,1)S(1)} %copy-done.10, s32[]{:T(128)S(6)} %copy.125, bf16[2,1280,3,64]{1,3,2,0:T(8,128)(2,1)S(1)} %copy-done.2), kind=kOutput, calls=%fused_computation.26.clone.1 | convolution fusion | flops 638972160 | bytes 40321024 | tf_op jit(solution)/shard_map/while/body/eval_jaxpr/qhd,khd->hqk/dot_general | solution.py:51
  345.2 13.8 %multiply_convert_fusion.5 = bf16[3,1280,1280]{1,2,0:T(8,128)(2,1)S(1)} fusion(f32[3,1280,1280]{1,2,0:T(8,128)} %get-tuple-element.336, f32[3,1280,1280]{1,2,0:T(8,128)} %fusion.127, f32[3,1280]{1,0:T(4,128)S(1)} %get-tuple-element.337), kind=kLoop, calls=%fused_computation.25.clone.1 | loop fusion | flops 14745600 | bytes 49167360 | tf_op jit(solution)/shard_map/while/body/eval_jaxpr/convert_element_type | solution.py:53
  368.6 3.8 stack.32
  375.5 3.8 stack.30
  382.4 3.8 stack.31
  389.9 6.3 constant_dynamic-slice_fusion.3
  399.9 16.1 %collective-permute-done.1 = bf16[640,3,1,192]{0,3,2,1:T(8,128)(2,1)S(1)} collective-permute-done((bf16[640,3,1,192]{0,3,2,1:T(8,128)(2,1)S(1)}, bf16[640,3,1,192]{0,3,2,1:T(8,128)(2,1)S(1)}, u32[]{:S(2)}, u32[]{:S(2)}) %collective-permute-start.1) | collective-permute-done | bytes 737312 | tf_op jit(solution)/shard_map/ppermute | solution.py:184
  417.1 13.6 %collective-permute-done.2 = bf16[640,3,1,192]{0,3,2,1:T(8,128)(2,1)S(1)} collective-permute-done((bf16[640,3,1,192]{0,3,2,1:T(8,128)(2,1)S(1)}, bf16[640,3,1,192]{0,3,2,1:T(8,128)(2,1)S(1)}, u32[]{:S(2)}, u32[]{:S(2)}) %collective-permute-start.2) | collective-permute-done | bytes 737312 | tf_op jit(solution)/shard_map/ppermute | solution.py:184
  431.9 6.9 pad_maximum_fusion
  440.8 4.3 gather_fusion
  449.0 5.3 fusion.62
  454.4 11.4 %fusion.65 = f32[3072,768]{0,1:T(8,128)} fusion(bf16[640,768]{1,0:T(8,128)(2,1)} %param.37, f32[640,3072]{1,0:T(8,128)} %copy-done.53, f32[3072]{0:T(1024)} %convert_element_type.121), kind=kOutput, calls=%fused_computation.136 | convolution fusion | flops 3039559680 | bytes 18296832 | tf_op jit(solution)/shard_map/nf,nd->fd/dot_general | solution.py:145
  466.4 10.6 %fusion.63 = f32[768,3072]{0,1:T(8,128)} fusion(bf16[640,3072]{1,0:T(8,128)(2,1)} %copy-done.54, f32[640,768]{1,0:T(8,128)} %copy-done.11, f32[768]{0:T(1024)} %convert_element_type.119, f32[768]{0:T(1024)S(1)} %copy-done.44, f32[640]{0:T(1024)} %copy-done.45, f32[640]{0:T(1024)S(1)} %copy-done.32), kind=kOutput, calls=%fused_computation.134 | convolution fusion | flops 3022356480 | bytes 15346688 | tf_op jit(solution)/shard_map/nd,nf->df/dot_general | solution.py:150
  477.7 11.6 %add_convert_fusion.1 = bf16[640,768]{1,0:T(8,128)(2,1)} fusion(f32[640,768]{1,0:T(8,128)} %copy-done.11, bf16[3072,768]{1,0:T(8,128)(2,1)} %param.35, f32[768]{0:T(1024)S(1)} %convert_element_type.123, f32[640,3072]{1,0:T(8,128)} %copy-done.53, f32[3072]{0:T(1024)} %convert_element_type.121), kind=kOutput, calls=%fused_computation.89 | convolution fusion | flops 3041034240 | bytes 15547392 | tf_op jit(solution)/shard_map/dot_general | solution.py:141
  492.0 6.7 multiply_reduce_fusion.2
  503.8 44.5 %all-reduce.9 = (f32[5,768]{1,0:T(8,128)}, f32[768]{0:T(1024)}, f32[768]{0:T(1024)}, f32[2,768]{1,0:T(2,128)}, f32[768]{0:T(1024)}, /*index=5*/f32[768]{0:T(1024)}, f32[768]{0:T(1024)}, f32[3072]{0:T(1024)}, f32[768]{0:T(1024)}) all-reduce(f32[5,768]{1,0:T(8,128)} %fusion.56, ...), channel_id=2, replica_groups=mesh['batch'=8,'head'=4] {'batch','head'}, use_global_device_ids=true, to_apply=%region_15.16.clone | all-reduce | flops 13056 | bytes 104448
  559.8 17.3 %reduce-scatter.7.cloned.1.call-done = f32[768,72]{0,1:T(8,128)} async-done(((f32[768,2304]{0,1:T(8,128)}), f32[768,72]{0,1:T(8,128)}) %reduce-scatter.7.cloned.1.call-update) | async-done | bytes 221200 | tf_op jit(solution)/shard_map/reduce_scatter | solution.py:208
  577.1 141.7 %reduce-scatter.13.cloned.1.call-done = f32[3072,24]{0,1:T(8,128)} async-done(((f32[3072,768]{0,1:T(8,128)}), f32[3072,24]{0,1:T(8,128)}) %reduce-scatter.13.cloned.1.call-update) | async-done | bytes 294928 | tf_op jit(solution)/shard_map/reduce_scatter | solution.py:216
  718.8 141.5 %reduce-scatter.11.cloned.1.call-done = f32[768,96]{0,1:T(8,128)} async-done(((f32[768,3072]{0,1:T(8,128)}), f32[768,96]{0,1:T(8,128)}) %reduce-scatter.11.cloned.1.call-update) | async-done | bytes 294928 | tf_op jit(solution)/shard_map/reduce_scatter | solution.py:214
  (254 shorter events, 126.9 us)
Async XLA Ops:
  7.2 6.1 copy-start
  8.0 4.7 copy-start.38
  8.9 3.8 copy-start.48
  26.7 40.7 %all-to-all-start = ((bf16[640,3,4,192]{0,3,1,2:T(8,128)(2,1)}), bf16[640,3,4,192]{0,3,1,2:T(8,128)(2,1)}, u32[]{:S(2)}, u32[]{:S(2)}) async-start(bf16[640,3,4,192]{0,3,1,2:T(8,128)(2,1)} %copy.66), calls=%async_computation | async-start | bytes 5898240 | tf_op jit(solution)/shard_map/all_to_all | solution.py:120
  84.8 6.6 copy-start.26
  115.4 10.9 %copy-start.23 = (f32[3,1280]{1,0:T(4,128)S(1)}, f32[3,1280]{1,0:T(4,128)}, u32[]{:S(2)}) copy-start(f32[3,1280]{1,0:T(4,128)} %get-tuple-element.325) | copy-start | bytes 46084 | tf_op jit(solution)/shard_map/while
  115.4 10.9 %copy-start.24 = (f32[3,1280]{1,0:T(4,128)S(1)}, f32[3,1280]{1,0:T(4,128)}, u32[]{:S(2)}) copy-start(f32[3,1280]{1,0:T(4,128)} %fusion.117) | copy-start | bytes 46084 | tf_op jit(solution)/shard_map/while
  115.4 10.9 %copy-start.27 = (f32[2,3,1280]{2,1,0:T(4,128)S(1)}, f32[2,3,1280]{2,1,0:T(4,128)}, u32[]{:S(2)}) copy-start(f32[2,3,1280]{2,1,0:T(4,128)} %get-tuple-element.348) | copy-start | bytes 92164 | tf_op jit(solution)/shard_map/while
  150.7 10.9 %copy-start.23 = (f32[3,1280]{1,0:T(4,128)S(1)}, f32[3,1280]{1,0:T(4,128)}, u32[]{:S(2)}) copy-start(f32[3,1280]{1,0:T(4,128)} %get-tuple-element.325) | copy-start | bytes 46084 | tf_op jit(solution)/shard_map/while
  150.7 10.9 %copy-start.24 = (f32[3,1280]{1,0:T(4,128)S(1)}, f32[3,1280]{1,0:T(4,128)}, u32[]{:S(2)}) copy-start(f32[3,1280]{1,0:T(4,128)} %fusion.117) | copy-start | bytes 46084 | tf_op jit(solution)/shard_map/while
  150.7 10.9 %copy-start.27 = (f32[2,3,1280]{2,1,0:T(4,128)S(1)}, f32[2,3,1280]{2,1,0:T(4,128)}, u32[]{:S(2)}) copy-start(f32[2,3,1280]{2,1,0:T(4,128)} %get-tuple-element.348) | copy-start | bytes 92164 | tf_op jit(solution)/shard_map/while
  171.9 18.0 %all-to-all-start.1 = ((bf16[4,640,192]{1,2,0:T(8,128)(2,1)}), bf16[4,640,192]{1,2,0:T(8,128)(2,1)}, u32[]{:S(2)}, u32[]{:S(2)}) async-start(bf16[4,640,192]{1,2,0:T(8,128)(2,1)} %copy.72), calls=%async_computation.1 | async-start | bytes 1966080 | tf_op jit(solution)/shard_map/all_to_all | solution.py:128
  176.8 36.0 %copy-start.43 = (f32[768]{0:T(1024)}, f32[768]{0:T(1024)S(1)}, u32[]{:S(2)}) copy-start(f32[768]{0:T(1024)S(1)} %convert_element_type.118) | copy-start | bytes 9220
  193.3 19.6 %copy-start.11 = (f32[640,768]{1,0:T(8,128)}, f32[640,768]{1,0:T(8,128)S(1)}, u32[]{:S(2)}) copy-start(f32[640,768]{1,0:T(8,128)S(1)} %get-tuple-element.223) | copy-start | bytes 5898244
  193.3 19.6 %copy-start.31 = (f32[640]{0:T(1024)}, f32[640]{0:T(1024)S(1)}, u32[]{:S(2)}) copy-start(f32[640]{0:T(1024)S(1)} %broadcast_multiply_fusion) | copy-start | bytes 7684
  193.3 6.8 slice-start.2
  193.7 19.2 %copy-start.45 = (f32[640]{0:T(1024)}, f32[640]{0:T(1024)S(1)}, u32[]{:S(2)}) copy-start(f32[640]{0:T(1024)S(1)} %fusion.60) | copy-start | bytes 7684
  193.7 6.4 copy-start.20
  193.7 6.4 copy-start.47
  193.7 6.4 slice-start.3
  193.8 15.0 %slice-start = ((s8[4718592]{0:T(1024)(128)(4,1)}), s8[4194304]{0:T(1024)(128)(4,1)S(1)}, s32[]{:S(2)}) async-start(s8[4718592]{0:T(1024)(128)(4,1)} %bitcast.191), calls=%async_computation.11 | async-start | bytes 8388608
  200.1 8.6 copy-start.53
  200.1 8.6 slice-start.1
  208.7 4.1 copy-start.54
  221.1 18.0 %all-to-all-start.2 = ((bf16[640,4,192]{0,2,1:T(8,128)(2,1)}), bf16[640,4,192]{0,2,1:T(8,128)(2,1)}, u32[]{:S(2)}, u32[]{:S(2)}) async-start(bf16[640,4,192]{0,2,1:T(8,128)(2,1)} %bitcast.182), calls=%async_computation.2 | async-start | bytes 1966080 | tf_op jit(solution)/shard_map/all_to_all | solution.py:164
  225.3 334.5 %reduce-scatter.9.cloned.1.call-start = ((), (), s32[]{:S(2)}) async-start(), calls=%async_computation.8 | async-start | bytes 2433024 | tf_op jit(solution)/shard_map/reduce_scatter | solution.py:210
  229.4 347.7 %reduce-scatter.7.cloned.1.call-start = ((), (), s32[]{:S(2)}) async-start(), calls=%async_computation.7 | async-start | bytes 7299072 | tf_op jit(solution)/shard_map/reduce_scatter | solution.py:208
  253.4 11.9 %copy-start.2 = (bf16[2,1280,3,64]{1,3,2,0:T(8,128)(2,1)S(1)}, bf16[2,1280,3,64]{1,3,2,0:T(8,128)(2,1)}, u32[]{:S(2)}) copy-start(bf16[2,1280,3,64]{1,3,2,0:T(8,128)(2,1)} %get-tuple-element.392) | copy-start | bytes 2949124 | tf_op jit(solution)/shard_map/while
  253.4 11.9 %copy-start.14 = (bf16[2,1280,3,64]{1,3,2,0:T(8,128)(2,1)S(1)}, bf16[2,1280,3,64]{1,3,2,0:T(8,128)(2,1)}, u32[]{:S(2)}) copy-start(bf16[2,1280,3,64]{1,3,2,0:T(8,128)(2,1)} %get-tuple-element.376) | copy-start | bytes 2949124 | tf_op jit(solution)/shard_map/while
  265.3 10.1 %copy-start.10 = (bf16[2,1280,3,64]{1,3,2,0:T(8,128)(2,1)S(1)}, bf16[2,1280,3,64]{1,3,2,0:T(8,128)(2,1)}, u32[]{:S(2)}) copy-start(bf16[2,1280,3,64]{1,3,2,0:T(8,128)(2,1)} %get-tuple-element.393) | copy-start | bytes 2949124 | tf_op jit(solution)/shard_map/while
  275.5 12.7 %copy-start.15 = (bf16[2,1280,3,64]{1,3,2,0:T(8,128)(2,1)}, bf16[2,1280,3,64]{1,3,2,0:T(8,128)(2,1)S(1)}, u32[]{:S(2)}) copy-start(bf16[2,1280,3,64]{1,3,2,0:T(8,128)(2,1)S(1)} %fusion.130) | copy-start | bytes 2949124 | tf_op jit(solution)/shard_map/while
  288.2 14.1 %copy-start.8 = (bf16[2,1280,3,64]{1,3,2,0:T(8,128)(2,1)S(1)}, bf16[2,1280,3,64]{1,3,2,0:T(8,128)(2,1)}, u32[]{:S(2)}) copy-start(bf16[2,1280,3,64]{1,3,2,0:T(8,128)(2,1)} %get-tuple-element.390) | copy-start | bytes 2949124 | tf_op jit(solution)/shard_map/while
  288.2 14.1 %copy-start.16 = (bf16[2,1280,3,64]{1,3,2,0:T(8,128)(2,1)S(1)}, bf16[2,1280,3,64]{1,3,2,0:T(8,128)(2,1)}, u32[]{:S(2)}) copy-start(bf16[2,1280,3,64]{1,3,2,0:T(8,128)(2,1)} %get-tuple-element.375) | copy-start | bytes 2949124 | tf_op jit(solution)/shard_map/while
  310.8 11.8 %copy-start.2 = (bf16[2,1280,3,64]{1,3,2,0:T(8,128)(2,1)S(1)}, bf16[2,1280,3,64]{1,3,2,0:T(8,128)(2,1)}, u32[]{:S(2)}) copy-start(bf16[2,1280,3,64]{1,3,2,0:T(8,128)(2,1)} %get-tuple-element.392) | copy-start | bytes 2949124 | tf_op jit(solution)/shard_map/while
  310.8 11.8 %copy-start.14 = (bf16[2,1280,3,64]{1,3,2,0:T(8,128)(2,1)S(1)}, bf16[2,1280,3,64]{1,3,2,0:T(8,128)(2,1)}, u32[]{:S(2)}) copy-start(bf16[2,1280,3,64]{1,3,2,0:T(8,128)(2,1)} %get-tuple-element.376) | copy-start | bytes 2949124 | tf_op jit(solution)/shard_map/while
  322.6 9.9 %copy-start.10 = (bf16[2,1280,3,64]{1,3,2,0:T(8,128)(2,1)S(1)}, bf16[2,1280,3,64]{1,3,2,0:T(8,128)(2,1)}, u32[]{:S(2)}) copy-start(bf16[2,1280,3,64]{1,3,2,0:T(8,128)(2,1)} %get-tuple-element.393) | copy-start | bytes 2949124 | tf_op jit(solution)/shard_map/while
  332.5 12.7 %copy-start.15 = (bf16[2,1280,3,64]{1,3,2,0:T(8,128)(2,1)}, bf16[2,1280,3,64]{1,3,2,0:T(8,128)(2,1)S(1)}, u32[]{:S(2)}) copy-start(bf16[2,1280,3,64]{1,3,2,0:T(8,128)(2,1)S(1)} %fusion.130) | copy-start | bytes 2949124 | tf_op jit(solution)/shard_map/while
  345.2 13.8 %copy-start.8 = (bf16[2,1280,3,64]{1,3,2,0:T(8,128)(2,1)S(1)}, bf16[2,1280,3,64]{1,3,2,0:T(8,128)(2,1)}, u32[]{:S(2)}) copy-start(bf16[2,1280,3,64]{1,3,2,0:T(8,128)(2,1)} %get-tuple-element.390) | copy-start | bytes 2949124 | tf_op jit(solution)/shard_map/while
  345.2 13.9 %copy-start.16 = (bf16[2,1280,3,64]{1,3,2,0:T(8,128)(2,1)S(1)}, bf16[2,1280,3,64]{1,3,2,0:T(8,128)(2,1)}, u32[]{:S(2)}) copy-start(bf16[2,1280,3,64]{1,3,2,0:T(8,128)(2,1)} %get-tuple-element.375) | copy-start | bytes 2949124 | tf_op jit(solution)/shard_map/while
  396.5 2.3 collective-permute-start
  396.6 19.4 %collective-permute-start.1 = (bf16[640,3,1,192]{0,3,2,1:T(8,128)(2,1)S(1)}, bf16[640,3,1,192]{0,3,2,1:T(8,128)(2,1)S(1)}, u32[]{:S(2)}, u32[]{:S(2)}) collective-permute-start(bf16[640,3,1,192]{0,3,2,1:T(8,128)(2,1)S(1)} %bitcast.185), channel_id=1, source_target_pairs={{0,2},{1,3},{2,0},{3,1},{4,6},{5,7},{6,4},{7,5},{8,10},{9,11},{10,... | collective-permute-start | bytes 2211848 | tf_op jit(solution)/shard_map/ppermute | solution.py:184
  397.1 33.6 %collective-permute-start.2 = (bf16[640,3,1,192]{0,3,2,1:T(8,128)(2,1)S(1)}, bf16[640,3,1,192]{0,3,2,1:T(8,128)(2,1)S(1)}, u32[]{:S(2)}, u32[]{:S(2)}) collective-permute-start(bf16[640,3,1,192]{0,3,2,1:T(8,128)(2,1)S(1)} %bitcast.187), channel_id=1, source_target_pairs={{0,3},{1,2},{2,1},{3,0},{4,7},{5,6},{6,5},{7,4},{8,11},{9,10},{10,... | collective-permute-start | bytes 2211848 | tf_op jit(solution)/shard_map/ppermute | solution.py:184
  454.3 264.5 %reduce-scatter.13.cloned.1.call-start = ((), (), s32[]{:S(2)}) async-start(), calls=%async_computation.10 | async-start | bytes 9732096 | tf_op jit(solution)/shard_map/reduce_scatter | solution.py:216
  465.8 394.5 %reduce-scatter.11.cloned.1.call-start = ((), (), s32[]{:S(2)}) async-start(), calls=%async_computation.9 | async-start | bytes 9732096 | tf_op jit(solution)/shard_map/reduce_scatter | solution.py:214
  477.7 11.6 %copy-start.1 = (bf16[4,640,3,192]{1,3,2,0:T(8,128)(2,1)S(1)}, bf16[4,640,3,192]{1,3,2,0:T(8,128)(2,1)}, u32[]{:S(2)}) copy-start(bf16[4,640,3,192]{1,3,2,0:T(8,128)(2,1)} %gather_fusion) | copy-start | bytes 8847364
  491.9 6.7 copy-start.34
  492.0 6.7 copy-start.5
  492.0 6.7 copy-start.42
  (35 other events, 72.2 us)
Sparse Core Ops, SparseCore 0:
  232.0 102.1 reduce-scatter.8
  454.4 122.6 reduce-scatter.6
  583.6 135.1 reduce-scatter.12
  725.1 135.1 reduce-scatter.10
